TPU v7x, 128 devices: a whole 4x4x4 slice. The times are simulated.
128 devices in a mesh: row: 16 (over y, z), col: 8 (over x, core).
Axes of the slice: x: 4, y: 4, z: 4, core: 2. Of those that a mesh axis runs over, the one named last changes fastest.
Arguments:
- blocks: bfloat16 [16, 8, 128, 4096], P('row', 'col'), may hold values from -0.25 to 0.25
- block_row: int32 [16, 8, 128], P('row', 'col'), may hold values from 0 to 15
- block_col: int32 [16, 8, 128], P('row', 'col'), may hold values from 0 to 31
- counts: int32 [16, 8], P('row', 'col'), may hold values from 0 to 128, as said below
- vectors: float32 [256, 4096], P(('col', 'row')), may hold values from -6 to 6
- row_mass: float32 [256, 64], P(('row', 'col')), may hold values from 0.25 to 4
- col_mass: float32 [256, 64], P(('col', 'row')), may hold values from 0.25 to 4
Outputs:
- subspace: float32 [256, 4096], P(('col', 'row'))
Inputs may be any that keep to these rules, and one draw needn't show every extreme that they name: `counts`: in every row panel one tile uses all 128 slots; every other tile uses at most 8.
All inputs are finite; a program needn't handle non-finite values.
Results may differ from a plain program's by a relative error of at most 0.0085.
Values may be sent and summed in bfloat16 or wider, within the bound.
A program may use at most 64 MiB of HBM per device.

v0:
```python
import jax
import jax.numpy as jnp
from jax import lax
from jax.sharding import PartitionSpec as P

ITERS = 4


def rotate(projected, gram):
    lower = jnp.linalg.cholesky(gram)
    inverse = lax.linalg.triangular_solve(
        lower, jnp.eye(gram.shape[0], dtype=jnp.float32), left_side=True, lower=True
    )
    return jnp.einsum(
        "kl,bli->bki",
        inverse,
        projected,
        precision=lax.Precision.HIGHEST,
        preferred_element_type=jnp.float32,
    )


def local_gram(projected):
    return jnp.einsum(
        "bki,bli->kl",
        projected,
        projected,
        precision=lax.Precision.HIGHEST,
        preferred_element_type=jnp.float32,
    )


def per_device(blocks, block_row, block_col, counts, vectors, row_mass, col_mass):
    tile = blocks[0, 0]
    n_cap = tile.shape[0]
    bsize = row_mass.shape[1]
    vecs = vectors.shape[1] // bsize
    own = vectors.shape[0]
    n_row = lax.axis_size("row")
    n_col = lax.axis_size("col")
    row_panel = own * n_col
    col_panel = own * n_row
    total_boxes = float(own * bsize * n_row * n_col)
    rows_idx = block_row[0, 0]
    cols_idx = block_col[0, 0]
    live = jnp.arange(n_cap) < counts[0, 0]
    fwd_ids = jnp.where(live, rows_idx, row_panel)
    bwd_ids = jnp.where(live, cols_idx, col_panel)
    square = tile.reshape(n_cap, bsize, bsize)
    inv_col = 1.0 / jnp.sqrt(col_mass)
    current = vectors.reshape(own, vecs, bsize)
    for step in range(ITERS):
        scaled = (current * inv_col[:, None, :]).astype(jnp.bfloat16).reshape(own, vecs * bsize)
        panel = lax.all_gather(scaled, "row", axis=0, tiled=True)
        forward_taken = jnp.take(panel.reshape(col_panel, vecs, bsize), cols_idx, axis=0)
        forward_product = jnp.einsum(
            "bij,bkj->bki", square, forward_taken, preferred_element_type=jnp.float32
        )
        forward_summed = jax.ops.segment_sum(forward_product, fwd_ids, num_segments=row_panel + 1)
        rows_sum = lax.psum_scatter(
            forward_summed[:row_panel].reshape(row_panel, vecs * bsize),
            "col",
            scatter_dimension=0,
            tiled=True,
        )
        weighted = (rows_sum.reshape(own, vecs, bsize) * row_mass[:, None, :]).astype(jnp.bfloat16)
        whole_rows = lax.all_gather(weighted.reshape(own, vecs * bsize), "col", axis=0, tiled=True)
        taken = jnp.take(whole_rows.reshape(row_panel, vecs, bsize), rows_idx, axis=0)
        product = jnp.einsum("bij,bki->bkj", square, taken, preferred_element_type=jnp.float32)
        summed = jax.ops.segment_sum(product, bwd_ids, num_segments=col_panel + 1)
        cols_sum = lax.psum_scatter(
            summed[:col_panel].reshape(col_panel, vecs * bsize),
            "row",
            scatter_dimension=0,
            tiled=True,
        )
        projected = cols_sum.reshape(own, vecs, bsize) * inv_col[:, None, :]
        gram = lax.psum(local_gram(projected), ("row", "col")) / total_boxes
        current = rotate(projected, gram)
    return current.reshape(own, vecs * bsize)


def solution(mesh):
    in_specs = (
        P("row", "col", None, None),
        P("row", "col", None),
        P("row", "col", None),
        P("row", "col"),
        P(("col", "row"), None),
        P(("row", "col"), None),
        P(("col", "row"), None),
    )
    out_specs = P(("col", "row"), None)
    return jax.shard_map(
        per_device, mesh=mesh, in_specs=in_specs, out_specs=out_specs, check_vma=False
    )
```

profile of v0, /device:TPU:1, one launch (start us, length us, event | category | flops | bytes accessed | tf_op | source)
XLA Modules:
  0.0 1238.8 jit_solution(7338653672180758130)
XLA Ops:
  9.4 20.8 %all-gather = bf16[16,2,4096]{2,1,0:T(2,128)(2,1)S(1)} all-gather(bf16[1,2,4096]{2,1,0:T(2,128)(2,1)S(1)} %fusion.66), channel_id=1, replica_groups=mesh['row'=16,'col'=8] {'row'}, dimensions={0}, use_global_device_ids=true | all-gather | bytes 278528 | tf_op jit(solution)/shard_map/all_gather | solution.py:54
  60.6 60.9 %all-reduce.17.cloned.1.call-done = f32[16,4096]{1,0:T(8,128)} async-done(((f32[16,4096]{1,0:T(8,128)}), f32[16,4096]{1,0:T(8,128)}) %all-reduce.17.cloned.1.call-update) | async-done | bytes 262160
  122.4 15.3 %all-gather.1 = bf16[8,2,4096]{2,1,0:T(2,128)(2,1)S(1)} all-gather(bf16[1,2,4096]{2,1,0:T(2,128)(2,1)S(1)} %fusion.67), channel_id=1, replica_groups=mesh['row'=16,'col'=8] {'col'}, dimensions={0}, use_global_device_ids=true | all-gather | bytes 147456 | tf_op jit(solution)/shard_map/all_gather | solution.py:67
  144.5 13.6 %scatter_fusion.1 = f32[33,64,64]{2,1,0:T(8,128)S(1)} fusion(f32[33,64,64]{2,1,0:T(8,128)S(1)} %broadcast.94.clone.2, s32[128]{0:T(128)S(1)} %get-tuple-element.17, f32[128,64,64]{2,1,0:T(8,128)} %fusion.12), kind=kCustom, calls=%fused_computation.9 | custom fusion | flops 524288 | bytes 6291968 | tf_op jit(solution)/shard_map/scatter-add | solution.py:70
  163.0 82.1 %all-reduce.19.cloned.1.call-done = f32[32,4096]{1,0:T(8,128)} async-done(((f32[32,4096]{1,0:T(8,128)}), f32[32,4096]{1,0:T(8,128)}) %all-reduce.19.cloned.1.call-update) | async-done | bytes 524304
  246.3 65.6 %psum.28 = f32[64,64]{0,1:T(8,128)S(1)} all-reduce(f32[64,64]{0,1:T(8,128)S(1)} %convolution_bitcast_fusion.8), channel_id=1, replica_groups=mesh['row'=16,'col'=8] {'row','col'}, use_global_device_ids=true, to_apply=%region_4.7 | all-reduce | flops 4096 | bytes 32768 | tf_op jit(solution)/shard_map/psum | solution.py:78
  325.0 16.8 %all-gather.2 = bf16[16,2,4096]{2,1,0:T(2,128)(2,1)S(1)} all-gather(bf16[1,2,4096]{2,1,0:T(2,128)(2,1)S(1)} %reshape.324), channel_id=1, replica_groups=mesh['row'=16,'col'=8] {'row'}, dimensions={0}, use_global_device_ids=true | all-gather | bytes 278528 | tf_op jit(solution)/shard_map/all_gather | solution.py:54
  363.8 60.7 %all-reduce.21.cloned.1.call-done = f32[16,4096]{1,0:T(8,128)} async-done(((f32[16,4096]{1,0:T(8,128)}), f32[16,4096]{1,0:T(8,128)}) %all-reduce.21.cloned.1.call-update) | async-done | bytes 262160
  425.4 15.3 %all-gather.3 = bf16[8,2,4096]{2,1,0:T(2,128)(2,1)S(1)} all-gather(bf16[1,2,4096]{2,1,0:T(2,128)(2,1)S(1)} %fusion.68), channel_id=1, replica_groups=mesh['row'=16,'col'=8] {'col'}, dimensions={0}, use_global_device_ids=true | all-gather | bytes 147456 | tf_op jit(solution)/shard_map/all_gather | solution.py:67
  447.5 13.6 %scatter_fusion.3 = f32[33,64,64]{2,1,0:T(8,128)S(1)} fusion(f32[33,64,64]{2,1,0:T(8,128)S(1)} %broadcast.94.clone.1, s32[128]{0:T(128)S(1)} %get-tuple-element.17, f32[128,64,64]{2,1,0:T(8,128)} %fusion.8), kind=kCustom, calls=%fused_computation.11 | custom fusion | flops 524288 | bytes 6291968 | tf_op jit(solution)/shard_map/scatter-add | solution.py:70
  464.7 83.4 %all-reduce.23.cloned.1.call-done = f32[32,4096]{1,0:T(8,128)} async-done(((f32[32,4096]{1,0:T(8,128)}), f32[32,4096]{1,0:T(8,128)}) %all-reduce.23.cloned.1.call-update) | async-done | bytes 524304
  549.3 65.6 %psum.29 = f32[64,64]{0,1:T(8,128)S(1)} all-reduce(f32[64,64]{0,1:T(8,128)S(1)} %convolution_bitcast_fusion.6), channel_id=1, replica_groups=mesh['row'=16,'col'=8] {'row','col'}, use_global_device_ids=true, to_apply=%region_11.16 | all-reduce | flops 4096 | bytes 32768 | tf_op jit(solution)/shard_map/psum | solution.py:78
  628.0 16.5 %all-gather.4 = bf16[16,2,4096]{2,1,0:T(2,128)(2,1)S(1)} all-gather(bf16[1,2,4096]{2,1,0:T(2,128)(2,1)S(1)} %reshape.328), channel_id=1, replica_groups=mesh['row'=16,'col'=8] {'row'}, dimensions={0}, use_global_device_ids=true | all-gather | bytes 278528 | tf_op jit(solution)/shard_map/all_gather | solution.py:54
  666.5 60.7 %all-reduce.25.cloned.1.call-done = f32[16,4096]{1,0:T(8,128)} async-done(((f32[16,4096]{1,0:T(8,128)}), f32[16,4096]{1,0:T(8,128)}) %all-reduce.25.cloned.1.call-update) | async-done | bytes 262160
  728.1 15.3 %all-gather.5 = bf16[8,2,4096]{2,1,0:T(2,128)(2,1)S(1)} all-gather(bf16[1,2,4096]{2,1,0:T(2,128)(2,1)S(1)} %fusion.69), channel_id=1, replica_groups=mesh['row'=16,'col'=8] {'col'}, dimensions={0}, use_global_device_ids=true | all-gather | bytes 147456 | tf_op jit(solution)/shard_map/all_gather | solution.py:67
  750.2 13.6 %scatter_fusion.5 = f32[33,64,64]{2,1,0:T(8,128)S(1)} fusion(f32[33,64,64]{2,1,0:T(8,128)S(1)} %broadcast.94.clone, s32[128]{0:T(128)S(1)} %get-tuple-element.17, f32[128,64,64]{2,1,0:T(8,128)} %fusion.4), kind=kCustom, calls=%fused_computation.13 | custom fusion | flops 524288 | bytes 6291968 | tf_op jit(solution)/shard_map/scatter-add | solution.py:70
  767.3 83.4 %all-reduce.27.cloned.1.call-done = f32[32,4096]{1,0:T(8,128)} async-done(((f32[32,4096]{1,0:T(8,128)}), f32[32,4096]{1,0:T(8,128)}) %all-reduce.27.cloned.1.call-update) | async-done | bytes 524304
  852.0 65.6 %psum.30 = f32[64,64]{0,1:T(8,128)S(1)} all-reduce(f32[64,64]{0,1:T(8,128)S(1)} %convolution_bitcast_fusion.4), channel_id=1, replica_groups=mesh['row'=16,'col'=8] {'row','col'}, use_global_device_ids=true, to_apply=%region_16.21 | all-reduce | flops 4096 | bytes 32768 | tf_op jit(solution)/shard_map/psum | solution.py:78
  930.7 16.5 %all-gather.6 = bf16[16,2,4096]{2,1,0:T(2,128)(2,1)S(1)} all-gather(bf16[1,2,4096]{2,1,0:T(2,128)(2,1)S(1)} %reshape.332), channel_id=1, replica_groups=mesh['row'=16,'col'=8] {'row'}, dimensions={0}, use_global_device_ids=true | all-gather | bytes 278528 | tf_op jit(solution)/shard_map/all_gather | solution.py:54
  969.2 60.7 %all-reduce.29.cloned.1.call-done = f32[16,4096]{1,0:T(8,128)} async-done(((f32[16,4096]{1,0:T(8,128)}), f32[16,4096]{1,0:T(8,128)}) %all-reduce.29.cloned.1.call-update) | async-done | bytes 262160
  1030.8 15.3 %all-gather.7 = bf16[8,2,4096]{2,1,0:T(2,128)(2,1)S(1)} all-gather(bf16[1,2,4096]{2,1,0:T(2,128)(2,1)S(1)} %fusion.70), channel_id=1, replica_groups=mesh['row'=16,'col'=8] {'col'}, dimensions={0}, use_global_device_ids=true | all-gather | bytes 147456 | tf_op jit(solution)/shard_map/all_gather | solution.py:67
  1052.9 13.6 %scatter_fusion.7 = f32[33,64,64]{2,1,0:T(8,128)S(1)} fusion(f32[33,64,64]{2,1,0:T(8,128)S(1)} %broadcast.94, s32[128]{0:T(128)S(1)} %get-tuple-element.17, f32[128,64,64]{2,1,0:T(8,128)} %fusion), kind=kCustom, calls=%fused_computation.15 | custom fusion | flops 524288 | bytes 6291968 | tf_op jit(solution)/shard_map/scatter-add | solution.py:70
  1067.8 83.4 %all-reduce.31.cloned.1.call-done = f32[32,4096]{1,0:T(8,128)} async-done(((f32[32,4096]{1,0:T(8,128)}), f32[32,4096]{1,0:T(8,128)}) %all-reduce.31.cloned.1.call-update) | async-done | bytes 524304
  1152.5 65.6 %psum.31 = f32[64,64]{0,1:T(8,128)S(1)} all-reduce(f32[64,64]{0,1:T(8,128)S(1)} %convolution_bitcast_fusion.2), channel_id=1, replica_groups=mesh['row'=16,'col'=8] {'row','col'}, use_global_device_ids=true, to_apply=%region_21.26 | all-reduce | flops 4096 | bytes 32768 | tf_op jit(solution)/shard_map/psum | solution.py:78
  (167 shorter events, 198.4 us)
Async XLA Ops:
  6.5 115.0 %all-reduce.17.cloned.1.call-start = ((), (), s32[]{:S(2)}) async-start(), calls=%async_computation | async-start | bytes 524288
  37.5 2.2 copy-start.1
  37.5 2.2 copy-start.2
  58.2 1.1 copy-start
  58.2 1.2 copy-start.4
  59.2 185.9 %all-reduce.19.cloned.1.call-start = ((), (), s32[]{:S(2)}) async-start(), calls=%async_computation.1 | async-start | bytes 1048576
  158.2 3.5 copy-start.3
  161.7 262.8 %all-reduce.21.cloned.1.call-start = ((), (), s32[]{:S(2)}) async-start(), calls=%async_computation.2 | async-start | bytes 524288
  363.7 184.3 %all-reduce.23.cloned.1.call-start = ((), (), s32[]{:S(2)}) async-start(), calls=%async_computation.3 | async-start | bytes 1048576
  464.6 262.6 %all-reduce.25.cloned.1.call-start = ((), (), s32[]{:S(2)}) async-start(), calls=%async_computation.4 | async-start | bytes 524288
  666.4 184.3 %all-reduce.27.cloned.1.call-start = ((), (), s32[]{:S(2)}) async-start(), calls=%async_computation.5 | async-start | bytes 1048576
  767.3 262.6 %all-reduce.29.cloned.1.call-start = ((), (), s32[]{:S(2)}) async-start(), calls=%async_computation.6 | async-start | bytes 524288
  969.1 182.1 %all-reduce.31.cloned.1.call-start = ((), (), s32[]{:S(2)}) async-start(), calls=%async_computation.7 | async-start | bytes 1048576
Sparse Core Ops, SparseCore 0:
  59.3 62.1 all-reduce.16
  161.8 83.2 all-reduce.18
  363.8 60.5 all-reduce.20
  464.7 83.2 all-reduce.22
  666.5 60.5 all-reduce.24
  767.4 83.2 all-reduce.26
  969.2 60.5 all-reduce.28
  1067.9 83.2 all-reduce.30
where the time goes:
time: 1250 us; the launch traced here: 1240 us
  waiting for transfers between devices  575 us (46%)
  blocking collectives  394 us (32%)
  other arithmetic  167 us (13%)
  local copies, waits for them, and re-layouts  46.5 us (4%)
  matrix products  39.1 us (3%)
  between operations  16.3 us (1%)
    unnamed x16, waiting for transfers between devices  575 us
    psum x4, blocking collectives, per_device(): gram = lax.psum(local_gram(projected), ('row', 'col')) / total_boxes  262 us
    all_gather x4, blocking collectives, per_device(): panel = lax.all_gather(scaled, 'row', axis=0, tiled=True)  70.7 us
    all_gather x4, blocking collectives, per_device(): lax.all_gather(weighted.reshape(own, vecs * bsize), 'col', axis=0, tiled=...  61.3 us
    scatter-add x4, other arithmetic, per_device(): summed = jax.ops.segment_sum(product, bwd_ids, num_segments=col_panel + 1)  54.5 us
    scatter-add x4, other arithmetic, per_device(): jax.ops.segment_sum(forward_product, fwd_ids, num_segments=row_panel + 1)  54.5 us
    another operation x12, other arithmetic, rotate(): lower = jnp.linalg.cholesky(gram)  26.1 us
  transfers between devices with their start and end apart: 8, of which 8 were waited for; matrix products, arithmetic and copies ran while one was open for 0% of the time, Pallas kernels for 0%

commit v1 on v0

--- a/solution.py
+++ b/solution.py
@@ -47,37 +47,29 @@
     fwd_ids = jnp.where(live, rows_idx, row_panel)
     bwd_ids = jnp.where(live, cols_idx, col_panel)
     square = tile.reshape(n_cap, bsize, bsize)
-    inv_col = 1.0 / jnp.sqrt(col_mass)
-    current = vectors.reshape(own, vecs, bsize)
+    col_mass_panel = lax.all_gather(col_mass, "row", axis=0, tiled=True)
+    row_mass_panel = lax.all_gather(row_mass, "col", axis=0, tiled=True)
+    inv_col = 1.0 / jnp.sqrt(col_mass_panel)
+    current = lax.all_gather(vectors, "row", axis=0, tiled=True).reshape(col_panel, vecs, bsize)
     for step in range(ITERS):
-        scaled = (current * inv_col[:, None, :]).astype(jnp.bfloat16).reshape(own, vecs * bsize)
-        panel = lax.all_gather(scaled, "row", axis=0, tiled=True)
-        forward_taken = jnp.take(panel.reshape(col_panel, vecs, bsize), cols_idx, axis=0)
+        scaled = (current * inv_col[:, None, :]).astype(jnp.bfloat16)
+        forward_taken = jnp.take(scaled, cols_idx, axis=0)
         forward_product = jnp.einsum(
             "bij,bkj->bki", square, forward_taken, preferred_element_type=jnp.float32
         )
         forward_summed = jax.ops.segment_sum(forward_product, fwd_ids, num_segments=row_panel + 1)
-        rows_sum = lax.psum_scatter(
-            forward_summed[:row_panel].reshape(row_panel, vecs * bsize),
-            "col",
-            scatter_dimension=0,
-            tiled=True,
-        )
-        weighted = (rows_sum.reshape(own, vecs, bsize) * row_mass[:, None, :]).astype(jnp.bfloat16)
-        whole_rows = lax.all_gather(weighted.reshape(own, vecs * bsize), "col", axis=0, tiled=True)
-        taken = jnp.take(whole_rows.reshape(row_panel, vecs, bsize), rows_idx, axis=0)
+        rows_sum = lax.psum(forward_summed[:row_panel], "col")
+        weighted = (rows_sum * row_mass_panel[:, None, :]).astype(jnp.bfloat16)
+        taken = jnp.take(weighted, rows_idx, axis=0)
         product = jnp.einsum("bij,bki->bkj", square, taken, preferred_element_type=jnp.float32)
         summed = jax.ops.segment_sum(product, bwd_ids, num_segments=col_panel + 1)
-        cols_sum = lax.psum_scatter(
-            summed[:col_panel].reshape(col_panel, vecs * bsize),
-            "row",
-            scatter_dimension=0,
-            tiled=True,
-        )
-        projected = cols_sum.reshape(own, vecs, bsize) * inv_col[:, None, :]
-        gram = lax.psum(local_gram(projected), ("row", "col")) / total_boxes
+        cols_sum = lax.psum(summed[:col_panel], "row")
+        projected = cols_sum * inv_col[:, None, :]
+        gram = lax.psum(local_gram(projected), "col") / total_boxes
         current = rotate(projected, gram)
-    return current.reshape(own, vecs * bsize)
+    me = lax.axis_index("row")
+    mine = lax.dynamic_slice_in_dim(current, me * own, own, 0)
+    return mine.reshape(own, vecs * bsize)
 
 
 def solution(mesh):

time: 1250 us -> 1010 us (0.81)
  blocking collectives: 394 us -> 153 us
  matrix products: 39.1 us -> 58.3 us
    unnamed x16 -> x8, waiting for transfers between devices: 575 us -> 0.13 us
    psum x0 -> x8, waiting for transfers between devices: none -> 568 us  [the longest x4 348 us: per_device(): cols_sum = lax.psum(summed[:col_panel], 'row')]
    psum x4, blocking collectives: 262 us -> 92.4 us  [per_device(): gram = lax.psum(local_gram(projected), 'col') / total_boxes]
    all_gather x8 -> x3, blocking collectives: 132 us -> 60.1 us  [the longest x1 22.1 us: per_device(): row_mass_panel = lax.all_gather(row_mass, 'col', axis=0, tiled=True)]
    reshape x25 -> x2, local copies, waits for them, and re-layouts: 15.6 us -> 2.33 us  [the longest x1 1.62 us: per_device(): lax.all_gather(vectors, 'row', axis=0, tiled=True)]
where the time goes in v1:
time: 1010 us; the launch traced here: 995 us
  waiting for transfers between devices  569 us (56%)
  other arithmetic  164 us (16%)
  blocking collectives  153 us (15%)
  matrix products  58.3 us (6%)
  local copies, waits for them, and re-layouts  36 us (4%)
  between operations  14.9 us (1%)
    psum x4, waiting for transfers between devices, per_device(): cols_sum = lax.psum(summed[:col_panel], 'row')  348 us
    psum x4, waiting for transfers between devices, per_device(): rows_sum = lax.psum(forward_summed[:row_panel], 'col')  220 us
    psum x4, blocking collectives, per_device(): gram = lax.psum(local_gram(projected), 'col') / total_boxes  92.4 us
    scatter-add x4, other arithmetic, per_device(): summed = jax.ops.segment_sum(product, bwd_ids, num_segments=col_panel + 1)  54.5 us
    scatter-add x4, other arithmetic, per_device(): jax.ops.segment_sum(forward_product, fwd_ids, num_segments=row_panel + 1)  54.5 us
    another operation x12, other arithmetic, rotate(): lower = jnp.linalg.cholesky(gram)  26.1 us
    another operation x8, other arithmetic, rotate(): lax.linalg.triangular_solve(lower, jnp.eye(gram.shape[0], dtype=jnp.float...  22.2 us
    all_gather x1, blocking collectives, per_device(): row_mass_panel = lax.all_gather(row_mass, 'col', axis=0, tiled=True)  22.1 us
  transfers between devices with their start and end apart: 8, of which 8 were waited for; matrix products, arithmetic and copies ran while one was open for 0% of the time, Pallas kernels for 0%

profile of v1, /device:TPU:1, one launch (start us, length us, event | category | flops | bytes accessed | tf_op | source)
XLA Modules:
  0.0 995.2 jit_solution(7439342869983005372)
XLA Ops:
  7.9 20.3 %all-gather.1 = f32[16,2,64]{2,1,0:T(2,128)S(1)} all-gather(f32[1,2,64]{2,1,0:T(2,128)} %bitcast.111), channel_id=1, replica_groups=mesh['row'=16,'col'=8] {'row'}, dimensions={0}, use_global_device_ids=true | all-gather | bytes 8704 | tf_op jit(solution)/shard_map/all_gather | solution.py:50
  28.3 17.7 %all-gather = f32[16,2,4096]{2,1,0:T(2,128)S(1)} all-gather(f32[1,2,4096]{2,1,0:T(2,128)} %bitcast.110), channel_id=1, replica_groups=mesh['row'=16,'col'=8] {'row'}, dimensions={0}, use_global_device_ids=true | all-gather | bytes 557056 | tf_op jit(solution)/shard_map/all_gather | solution.py:53
  60.3 13.6 %scatter_fusion = f32[17,64,64]{2,1,0:T(8,128)S(1)} fusion(f32[17,64,64]{2,1,0:T(8,128)S(1)} %broadcast.82.clone.2, s32[128]{0:T(128)S(1)} %get-tuple-element.8, f32[128,64,64]{2,1,0:T(8,128)} %fusion.14), kind=kCustom, calls=%fused_computation.8 | custom fusion | flops 524288 | bytes 6291968 | tf_op jit(solution)/shard_map/scatter-add | solution.py:60
  74.9 22.1 %all-gather.2 = f32[8,2,64]{2,1,0:T(2,128)S(1)} all-gather(f32[1,2,64]{2,1,0:T(2,128)S(1)} %bitcast.112), channel_id=1, replica_groups=mesh['row'=16,'col'=8] {'col'}, dimensions={0}, use_global_device_ids=true | all-gather | bytes 4608 | tf_op jit(solution)/shard_map/all_gather | solution.py:51
  97.0 46.0 %all-reduce.9.cloned.1.call-done = f32[16,64,64]{2,1,0:T(8,128)} async-done(((f32[16,64,64]{2,1,0:T(8,128)}), f32[16,64,64]{2,1,0:T(8,128)}) %all-reduce.9.cloned.1.call-update) | async-done | bytes 262160 | tf_op jit(solution)/shard_map/psum | solution.py:61
  150.7 13.6 %scatter_fusion.1 = f32[33,64,64]{2,1,0:T(8,128)S(1)} fusion(f32[33,64,64]{2,1,0:T(8,128)S(1)} %broadcast.81.clone.2, s32[128]{0:T(128)S(1)} %get-tuple-element.6, f32[128,64,64]{2,1,0:T(8,128)} %fusion.12), kind=kCustom, calls=%fused_computation.9 | custom fusion | flops 524288 | bytes 6291968 | tf_op jit(solution)/shard_map/scatter-add | solution.py:65
  165.5 87.1 %all-reduce.11.cloned.1.call-done = f32[32,64,64]{2,1,0:T(8,128)} async-done(((f32[32,64,64]{2,1,0:T(8,128)}), f32[32,64,64]{2,1,0:T(8,128)}) %all-reduce.11.cloned.1.call-update) | async-done | bytes 524304 | tf_op jit(solution)/shard_map/psum | solution.py:66
  255.3 23.3 %psum.86 = f32[64,64]{0,1:T(8,128)S(1)} all-reduce(f32[64,64]{0,1:T(8,128)S(1)} %convolution_bitcast_fusion.7), channel_id=1, replica_groups=mesh['row'=16,'col'=8] {'col'}, use_global_device_ids=true, to_apply=%region_4.7 | all-reduce | flops 4096 | bytes 32768 | tf_op jit(solution)/shard_map/psum | solution.py:68
  302.2 13.6 %scatter_fusion.2 = f32[17,64,64]{2,1,0:T(8,128)S(1)} fusion(f32[17,64,64]{2,1,0:T(8,128)S(1)} %broadcast.82.clone.1, s32[128]{0:T(128)S(1)} %get-tuple-element.8, f32[128,64,64]{2,1,0:T(8,128)} %fusion.10), kind=kCustom, calls=%fused_computation.10 | custom fusion | flops 524288 | bytes 6291968 | tf_op jit(solution)/shard_map/scatter-add | solution.py:60
  316.8 58.0 %all-reduce.13.cloned.1.call-done = f32[16,64,64]{2,1,0:T(8,128)} async-done(((f32[16,64,64]{2,1,0:T(8,128)}), f32[16,64,64]{2,1,0:T(8,128)}) %all-reduce.13.cloned.1.call-update) | async-done | bytes 262160 | tf_op jit(solution)/shard_map/psum | solution.py:61
  382.4 13.6 %scatter_fusion.3 = f32[33,64,64]{2,1,0:T(8,128)S(1)} fusion(f32[33,64,64]{2,1,0:T(8,128)S(1)} %broadcast.81.clone.1, s32[128]{0:T(128)S(1)} %get-tuple-element.6, f32[128,64,64]{2,1,0:T(8,128)} %fusion.8), kind=kCustom, calls=%fused_computation.11 | custom fusion | flops 524288 | bytes 6291968 | tf_op jit(solution)/shard_map/scatter-add | solution.py:65
  397.2 87.1 %all-reduce.15.cloned.1.call-done = f32[32,64,64]{2,1,0:T(8,128)} async-done(((f32[32,64,64]{2,1,0:T(8,128)}), f32[32,64,64]{2,1,0:T(8,128)}) %all-reduce.15.cloned.1.call-update) | async-done | bytes 524304 | tf_op jit(solution)/shard_map/psum | solution.py:66
  487.1 23.0 %psum.89 = f32[64,64]{0,1:T(8,128)S(1)} all-reduce(f32[64,64]{0,1:T(8,128)S(1)} %convolution_bitcast_fusion.5), channel_id=1, replica_groups=mesh['row'=16,'col'=8] {'col'}, use_global_device_ids=true, to_apply=%region_11.16 | all-reduce | flops 4096 | bytes 32768 | tf_op jit(solution)/shard_map/psum | solution.py:68
  510.2 5.8 cholesky.85
  533.6 13.6 %scatter_fusion.4 = f32[17,64,64]{2,1,0:T(8,128)S(1)} fusion(f32[17,64,64]{2,1,0:T(8,128)S(1)} %broadcast.82.clone, s32[128]{0:T(128)S(1)} %get-tuple-element.8, f32[128,64,64]{2,1,0:T(8,128)} %fusion.6), kind=kCustom, calls=%fused_computation.12 | custom fusion | flops 524288 | bytes 6291968 | tf_op jit(solution)/shard_map/scatter-add | solution.py:60
  548.2 58.0 %all-reduce.17.cloned.1.call-done = f32[16,64,64]{2,1,0:T(8,128)} async-done(((f32[16,64,64]{2,1,0:T(8,128)}), f32[16,64,64]{2,1,0:T(8,128)}) %all-reduce.17.cloned.1.call-update) | async-done | bytes 262160 | tf_op jit(solution)/shard_map/psum | solution.py:61
  613.8 13.6 %scatter_fusion.5 = f32[33,64,64]{2,1,0:T(8,128)S(1)} fusion(f32[33,64,64]{2,1,0:T(8,128)S(1)} %broadcast.81.clone, s32[128]{0:T(128)S(1)} %get-tuple-element.6, f32[128,64,64]{2,1,0:T(8,128)} %fusion.4), kind=kCustom, calls=%fused_computation.13 | custom fusion | flops 524288 | bytes 6291968 | tf_op jit(solution)/shard_map/scatter-add | solution.py:65
  628.6 87.1 %all-reduce.19.cloned.1.call-done = f32[32,64,64]{2,1,0:T(8,128)} async-done(((f32[32,64,64]{2,1,0:T(8,128)}), f32[32,64,64]{2,1,0:T(8,128)}) %all-reduce.19.cloned.1.call-update) | async-done | bytes 524304 | tf_op jit(solution)/shard_map/psum | solution.py:66
  718.5 23.0 %psum.92 = f32[64,64]{0,1:T(8,128)S(1)} all-reduce(f32[64,64]{0,1:T(8,128)S(1)} %convolution_bitcast_fusion.3), channel_id=1, replica_groups=mesh['row'=16,'col'=8] {'col'}, use_global_device_ids=true, to_apply=%region_16.21 | all-reduce | flops 4096 | bytes 32768 | tf_op jit(solution)/shard_map/psum | solution.py:68
  765.0 13.6 %scatter_fusion.6 = f32[17,64,64]{2,1,0:T(8,128)S(1)} fusion(f32[17,64,64]{2,1,0:T(8,128)S(1)} %broadcast.82, s32[128]{0:T(128)S(1)} %get-tuple-element.8, f32[128,64,64]{2,1,0:T(8,128)} %fusion.2), kind=kCustom, calls=%fused_computation.14 | custom fusion | flops 524288 | bytes 6291968 | tf_op jit(solution)/shard_map/scatter-add | solution.py:60
  779.6 58.0 %all-reduce.21.cloned.1.call-done = f32[16,64,64]{2,1,0:T(8,128)} async-done(((f32[16,64,64]{2,1,0:T(8,128)}), f32[16,64,64]{2,1,0:T(8,128)}) %all-reduce.21.cloned.1.call-update) | async-done | bytes 262160 | tf_op jit(solution)/shard_map/psum | solution.py:61
  845.2 13.6 %scatter_fusion.7 = f32[33,64,64]{2,1,0:T(8,128)S(1)} fusion(f32[33,64,64]{2,1,0:T(8,128)S(1)} %broadcast.81, s32[128]{0:T(128)S(1)} %get-tuple-element.6, f32[128,64,64]{2,1,0:T(8,128)} %fusion), kind=kCustom, calls=%fused_computation.15 | custom fusion | flops 524288 | bytes 6291968 | tf_op jit(solution)/shard_map/scatter-add | solution.py:65
  860.0 87.1 %all-reduce.23.cloned.1.call-done = f32[32,64,64]{2,1,0:T(8,128)} async-done(((f32[32,64,64]{2,1,0:T(8,128)}), f32[32,64,64]{2,1,0:T(8,128)}) %all-reduce.23.cloned.1.call-update) | async-done | bytes 524304 | tf_op jit(solution)/shard_map/psum | solution.py:66
  949.9 23.1 %psum.95 = f32[64,64]{0,1:T(8,128)S(1)} all-reduce(f32[64,64]{0,1:T(8,128)S(1)} %convolution_bitcast_fusion.1), channel_id=1, replica_groups=mesh['row'=16,'col'=8] {'col'}, use_global_device_ids=true, to_apply=%region_21.26 | all-reduce | flops 4096 | bytes 32768 | tf_op jit(solution)/shard_map/psum | solution.py:68
  (129 shorter events, 144.4 us)
Async XLA Ops:
  6.5 41.1 %copy-start.4 = (bf16[1,1,128,4096]{3,2,1,0:T(8,128)(2,1)S(1)}, bf16[1,1,128,4096]{3,2,1,0:T(8,128)(2,1)}, u32[]{:S(2)}) copy-start(bf16[1,1,128,4096]{3,2,1,0:T(8,128)(2,1)} %param.14) | copy-start | bytes 3145732
  6.5 136.5 %all-reduce.9.cloned.1.call-start = ((), (), s32[]{:S(2)}) async-start(), calls=%async_computation | async-start | bytes 1048576 | tf_op jit(solution)/shard_map/psum | solution.py:61
  53.3 2.2 copy-start.6
  53.3 2.2 copy-start.7
  60.3 14.6 %copy-start.5 = (f32[2,64]{1,0:T(2,128)S(1)}, f32[2,64]{1,0:T(2,128)}, u32[]{:S(2)}) copy-start(f32[2,64]{1,0:T(2,128)} %param.19) | copy-start | bytes 1540
  74.8 177.8 %all-reduce.11.cloned.1.call-start = ((), (), s32[]{:S(2)}) async-start(), calls=%async_computation.1 | async-start | bytes 2097152 | tf_op jit(solution)/shard_map/psum | solution.py:66
  165.5 209.3 %all-reduce.13.cloned.1.call-start = ((), (), s32[]{:S(2)}) async-start(), calls=%async_computation.2 | async-start | bytes 1048576 | tf_op jit(solution)/shard_map/psum | solution.py:61
  252.6 38.5 %copy-start.1 = (f32[32,64,64]{2,1,0:T(8,128)S(1)}, f32[32,64,64]{2,1,0:T(8,128)}, u32[]{:S(2)}) copy-start(f32[32,64,64]{2,1,0:T(8,128)} %all-reduce.11.cloned.1.call-done) | copy-start | bytes 1572868
  316.7 167.6 %all-reduce.15.cloned.1.call-start = ((), (), s32[]{:S(2)}) async-start(), calls=%async_computation.3 | async-start | bytes 2097152 | tf_op jit(solution)/shard_map/psum | solution.py:66
  397.2 209.0 %all-reduce.17.cloned.1.call-start = ((), (), s32[]{:S(2)}) async-start(), calls=%async_computation.4 | async-start | bytes 1048576 | tf_op jit(solution)/shard_map/psum | solution.py:61
  484.3 38.2 %copy-start.2 = (f32[32,64,64]{2,1,0:T(8,128)S(1)}, f32[32,64,64]{2,1,0:T(8,128)}, u32[]{:S(2)}) copy-start(f32[32,64,64]{2,1,0:T(8,128)} %all-reduce.15.cloned.1.call-done) | copy-start | bytes 1572868
  548.1 167.6 %all-reduce.19.cloned.1.call-start = ((), (), s32[]{:S(2)}) async-start(), calls=%async_computation.5 | async-start | bytes 2097152 | tf_op jit(solution)/shard_map/psum | solution.py:66
  628.6 209.0 %all-reduce.21.cloned.1.call-start = ((), (), s32[]{:S(2)}) async-start(), calls=%async_computation.6 | async-start | bytes 1048576 | tf_op jit(solution)/shard_map/psum | solution.py:61
  715.7 38.2 %copy-start.3 = (f32[32,64,64]{2,1,0:T(8,128)S(1)}, f32[32,64,64]{2,1,0:T(8,128)}, u32[]{:S(2)}) copy-start(f32[32,64,64]{2,1,0:T(8,128)} %all-reduce.19.cloned.1.call-done) | copy-start | bytes 1572868
  779.5 167.6 %all-reduce.23.cloned.1.call-start = ((), (), s32[]{:S(2)}) async-start(), calls=%async_computation.7 | async-start | bytes 2097152 | tf_op jit(solution)/shard_map/psum | solution.py:66
  947.2 38.3 %copy-start = (f32[32,64,64]{2,1,0:T(8,128)S(1)}, f32[32,64,64]{2,1,0:T(8,128)}, u32[]{:S(2)}) copy-start(f32[32,64,64]{2,1,0:T(8,128)} %all-reduce.23.cloned.1.call-done) | copy-start | bytes 1572868
Sparse Core Ops, SparseCore 0:
  74.9 68.0 all-reduce.8
  165.6 86.9 all-reduce.10
  316.8 57.9 all-reduce.12
  397.3 86.9 all-reduce.14
  548.2 57.9 all-reduce.16
  628.7 86.9 all-reduce.18
  779.6 57.9 all-reduce.20
  860.2 86.9 all-reduce.22
